TPU v7x, 32 devices: a whole 2x2x4 slice. The times are simulated.
32 devices in a mesh: row: 4 (over y, x), col: 4 (over z), cond: 2 (over core).
Axes of the slice: x: 2, y: 2, z: 4, core: 2. Of those that a mesh axis runs over, the one named last changes fastest.
Arguments:
- mask: float32 [512, 512], P('row', 'col'), may hold values from -1 to 1
- target: int32 [512, 512], P('row', 'col'), may hold values 0 or 1
- cond_index: int32 [4], P('cond'), may hold values from 0 to 7
- kernels: float32 [8, 2, 12, 576], replicated, may hold values from -6 to 6
- dose: float32 [8], replicated, may hold values from 0.7 to 1.4
Outputs:
- mask_grad: float32 [512, 512], P('row', 'col')
All inputs are finite; a program needn't handle non-finite values. No bound on the sum of `target` on one device may be relied on, other than what follows from the above.
Results may differ from a plain program's by a relative error of at most 0.0003.
Values sent between devices are 32-bit elements; how exact they have to be, the bound alone decides.
No kernel may reach another device: no remote copies, remote signals or barrier semaphores. Data moves between devices by JAX's collectives and lax.ppermute only.
A program may use at most 64 MiB of HBM per device.

v0:
```python
import functools
import math

import jax
import jax.numpy as jnp
import numpy as np
from jax import lax
from jax.experimental import pallas as pl
from jax.experimental.pallas import tpu as pltpu
from jax.sharding import PartitionSpec as P

MARGIN = 128
BAND = 24
STEEP = 4.0
THRESH = 0.6

HALF = 64
AXES = ("row", "col", "cond")
BF = jnp.bfloat16
F32 = jnp.float32


def pieces(table, count):
    out, rest = [], np.asarray(table, np.float32)
    for _ in range(count):
        part = rest.astype(BF)
        out.append(part)
        rest = rest - part.astype(np.float32)
    return out


def angles(left, right, period):
    left, right = np.asarray(left, np.int64), np.asarray(right, np.int64)
    return (left[:, None] * right[None, :] % period) * (2.0 * math.pi / period)


def frequencies():
    return np.arange(BAND) - BAND // 2


def lanes(*blocks):
    rows = blocks[0][1].shape[0]
    width = -(-max(at + block.shape[1] for at, block in blocks) // 128) * 128
    out = np.zeros((rows, width))
    for at, block in blocks:
        out[:, at : at + block.shape[1]] = block
    return out


def rows_at(height, *blocks):
    out = np.zeros((height, blocks[0][1].shape[1]))
    for at, block in blocks:
        out[at : at + block.shape[0]] = block
    return out


def three(table):
    high, low = pieces(table, 2)
    return np.concatenate([high, high, low], 1)


def stacked(table, count):
    return np.concatenate(pieces(table, count), 0)


def local_tables(tile, window):
    places = np.arange(tile)
    col_table = []
    for shift in (MARGIN, 0, 2 * MARGIN):
        phase = angles(places + shift, frequencies(), window)
        block = np.concatenate([np.cos(phase), -np.sin(phase)], 1) / window
        col_table.append(stacked(lanes((0, block), (HALF, block)), 2))
    phase = angles(frequencies(), places + MARGIN, window)
    row_table = three(np.concatenate([np.cos(phase), -np.sin(phase)], 0))
    phase = angles(frequencies(), np.full(HALF, MARGIN), window)
    cos, sin = np.cos(phase), np.sin(phase)
    turn = np.concatenate([np.concatenate([cos, cos], 1), np.concatenate([sin, -sin], 1)], 0)
    return np.concatenate(col_table, 0), row_table, turn.astype(np.float32)


def field_tables(tile, window):
    count = 2 * BAND
    points = np.arange(count)
    phase = angles(frequencies(), points, count)
    cos, sin = np.cos(phase), np.sin(phase)
    one = np.concatenate(
        [lanes((0, cos), (HALF, sin)), lanes((0, -sin), (HALF, cos)), np.zeros((HALF - count, 2 * HALF))]
    )
    none = np.zeros_like(one)
    to_cols = np.concatenate(
        [np.concatenate([one, none], 1), np.concatenate([none, one], 1)], 0
    )
    to_rows = np.concatenate([cos.T, -sin.T], 1)
    where = (np.arange(tile)[:, None] + MARGIN) / window - points[None, :] / count
    spread = np.ones((tile, count))
    for order in range(1, BAND):
        spread += 2.0 * np.cos(2.0 * math.pi * order * where)
    spread /= count
    spread_cols = rows_at(HALF, (0, spread.T))
    gather_cols = lanes((0, spread), (HALF, spread))
    from_rows = np.concatenate([cos, sin], 0)
    return (
        stacked(to_cols, 2),
        three(to_rows),
        stacked(spread_cols, 2),
        three(spread),
        three(spread.T),
        stacked(gather_cols, 2),
        three(from_rows),
        np.concatenate(pieces(to_cols.T, 2), 1),
    )


def adjoint_tables(tile, window):
    places = np.arange(tile) + MARGIN
    phase = angles(frequencies(), places, window)
    cos, sin = np.cos(phase), np.sin(phase)
    first = np.concatenate([cos, -sin], 1)
    second = np.concatenate([-sin, -cos], 1)
    cols = rows_at(
        2 * HALF, (0, first), (BAND, first), (HALF, second), (HALF + BAND, second)
    )
    rows = np.concatenate([cos.T, sin.T], 1) / window
    return stacked(cols, 2), three(rows)


def toward(at, core, line, size):
    onward = lax.rem(core + line, 2) == 0
    other = jnp.where(onward, at + 1, at - 1)
    return onward, (other >= 0) & (other < size)


def dot(left, right):
    return jnp.dot(left, right, preferred_element_type=F32)


def split(value, count):
    out, rest = [], value
    for step in range(count):
        part = rest.astype(BF)
        out.append(part)
        if step + 1 < count:
            rest = rest - part.astype(F32)
    return out


def lane_ids(shape):
    return lax.broadcasted_iota(jnp.int32, shape, len(shape) - 1)


def doubled(value):
    high = value.astype(BF).astype(F32)
    part = jnp.where(lane_ids(value.shape) < HALF, high, value - high).astype(BF)
    return jnp.concatenate([part, part], 1)


def four_weights(ref):
    size = ref.shape[0] // 2
    high, low = ref[:size], ref[size:]
    return jnp.concatenate([high, high, low, low], 0)


def three_right(value):
    high, low = split(value, 2)
    return jnp.concatenate([high, low, high], 0)


def fetch(sources, targets, sems):
    copies = [
        pltpu.make_async_copy(source, target, sems.at[at])
        for at, (source, target) in enumerate(zip(sources, targets))
    ]
    for copy in copies:
        copy.start()
    return copies


def local_spectrum(tile_value, col_table, row_table, turn):
    size = col_table.shape[0] // 2
    high, low = split(tile_value, 2)
    ch, cl = col_table[:size], col_table[size:]
    partial = dot(jnp.concatenate([high, low, high], 1), jnp.concatenate([ch, ch, cl], 0))
    both = dot(row_table, three_right(partial))
    lane = lane_ids((BAND, both.shape[1])) % HALF

    def times_i(value):
        return jnp.where(
            lane < BAND,
            -pltpu.roll(value, value.shape[1] - BAND, 1),
            jnp.where(lane < 2 * BAND, pltpu.roll(value, BAND, 1), 0.0),
        )

    centre = both[:BAND] + times_i(both[BAND:])
    ends = turn[:BAND] * centre + turn[BAND:] * times_i(centre)
    return jnp.concatenate([ends, centre], 0)


def open_kernel(*refs):
    cond_hbm, dose_hbm, mask_hbm, kernels_hbm = refs[:4]
    cond_ref, dose_ref, mask_ref, sems = refs[-4:]
    count = (len(refs) - 11) // 2
    sources, targets = refs[4 : 4 + count], refs[7 + count : 7 + 2 * count]
    own_ref, chosen_ref, strength_ref = refs[4 + count : 7 + count]
    conds = cond_hbm.shape[0]
    copies = []

    def start(source, target):
        copy = pltpu.make_async_copy(source, target, sems.at[len(copies)])
        copy.start()
        copies.append(copy)
        return copy

    scalars = [start(cond_hbm, cond_ref), start(dose_hbm, dose_ref)]
    first = [start(mask_hbm, mask_ref)]
    first += [start(source, target) for source, target in zip(sources[:3], targets[:3])]
    for copy in scalars:
        copy.wait()
    rest = [start(kernels_hbm.at[cond_ref[c]], chosen_ref.at[c]) for c in range(conds)]
    rest += [start(source, target) for source, target in zip(sources[3:], targets[3:])]
    for c in range(conds):
        strength_ref[c] = jnp.full(strength_ref.shape[1:], dose_ref[cond_ref[c]], F32)
    for copy in first:
        copy.wait()
    col_ref, row_ref, turn_ref = targets[:3]
    own_ref[...] = local_spectrum(
        mask_ref[...], col_ref[: 2 * mask_ref.shape[0]], row_ref[...], turn_ref[...]
    )
    for copy in rest:
        copy.wait()


def near_kernel(mesh_shape, tile_ref, col_ref, row_ref, turn_ref, out_ref):
    row, col, core = (lax.axis_index(name) for name in AXES)
    right, valid = toward(col, core, row, mesh_shape[1])
    size = 2 * tile_ref.shape[0]
    at = pl.multiple_of(jnp.where(right, 2 * size, size), size)
    share = local_spectrum(tile_ref[...], col_ref[pl.ds(at, size)], row_ref[...], turn_ref[...])
    out_ref[...] = jnp.where(valid, share, 0.0)


def arrange_kernel(real_ref, imag_ref, first_ref, second_ref):
    total = real_ref.shape[0] // BAND
    for pair in range(total // 2):
        first, second = 0.0, 0.0
        for part in range(2):
            at = (2 * pair + part) * BAND
            pad = jnp.zeros((BAND, 2 * HALF - BAND), F32)
            real = jnp.concatenate([real_ref[at : at + BAND, :], pad], 1)
            imag = jnp.concatenate([imag_ref[at : at + BAND, :], pad], 1)

            def moved(value, by):
                return pltpu.roll(value, part * HALF + by, 1) if part * HALF + by else value

            first = first + (moved(real, 0) + moved(imag, BAND))
            second = second + (moved(real, BAND) - moved(imag, 0))
        first_ref[:, pair * 2 * HALF : (pair + 1) * 2 * HALF] = first
        second_ref[:, pair * 2 * HALF : (pair + 1) * 2 * HALF] = second


def field_kernel(
    mesh_shape, strength_ref, own_ref, near_ref, far_ref, side_ref, other_ref,
    first_ref, second_ref, target_ref, to_cols_ref, to_rows_ref, spread_cols_ref, spread_ref,
    gather_rows_ref, gather_cols_ref, from_rows_ref, from_cols_ref, out_ref, rows_ref, field_ref,
):
    conds = strength_ref.shape[0]
    count = 2 * BAND
    pairs = first_ref.shape[1] // (2 * HALF)
    per = 2 * pairs // conds
    tile = target_ref.shape[0]
    wide = 4 * HALF
    row, col, core = (lax.axis_index(name) for name in AXES)

    def half(value, core):
        onward, valid = toward(row, core, col, mesh_shape[0])
        low_half = lane_ids(value.shape) < HALF
        kept = jnp.where(onward, jnp.where(low_half, 0.0, value), jnp.where(low_half, value, 0.0))
        kept = jnp.where(valid, kept, 0.0)
        return kept + pltpu.roll(kept, HALF, 1)

    spectrum = own_ref[BAND:] + near_ref[BAND:] + far_ref[BAND:]
    spectrum += half(side_ref[...], core) + half(other_ref[...], 1 - core)
    lane = lane_ids(spectrum.shape) % HALF
    real = jnp.where(lane < BAND, spectrum, 0.0)
    imag = jnp.where(lane >= BAND, spectrum, 0.0)
    real = real + pltpu.roll(real, BAND, 1)
    imag = imag + pltpu.roll(imag, 2 * HALF - BAND, 1)

    to_rows = to_rows_ref[...]
    for quad in range(pairs // 2):
        blocks = []
        for pair in (2 * quad, 2 * quad + 1):
            one = first_ref[:, pair * 2 * HALF : (pair + 1) * 2 * HALF]
            two = second_ref[:, pair * 2 * HALF : (pair + 1) * 2 * HALF]
            blocks.append(jnp.concatenate([one * real + two * imag, one * imag - two * real], 0))
        both = dot(to_rows, three_right(jnp.concatenate(blocks, 1)))
        for part in range(2):
            at = (2 * quad + part) * count
            rows_ref[at : at + count, :] = both[:, part * 2 * HALF : (part + 1) * 2 * HALF]

    weights = four_weights(to_cols_ref)
    chunk = rows_ref.shape[0] // 2
    for at in (0, chunk):
        high, low = split(rows_ref[at : at + chunk, :], 2)
        field_ref[at : at + chunk, :] = dot(jnp.concatenate([high, low, high, low], 1), weights)
    sums = [jnp.zeros((count, 2 * HALF), F32) for _ in range(conds)]
    for pair in range(pairs):
        both = field_ref[pair * count : (pair + 1) * count, :]
        squares = both * both
        for part in range(2):
            c = (2 * pair + part) // per
            sums[c] = sums[c] + squares[:, part * 2 * HALF : (part + 1) * 2 * HALF]

    coarse = jnp.concatenate([value + pltpu.roll(value, HALF, 1) for value in sums], 0)
    lines = dot(doubled(coarse), four_weights(spread_cols_ref))
    right = jnp.concatenate(
        [three_right(lines[c * count : (c + 1) * count]) for c in range(conds)], 1
    )
    image = dot(spread_ref[...], right)

    goal = target_ref[...].astype(F32)
    norm = 1.0 / (per * BAND * BAND)
    slopes = []
    for c in range(conds):
        strength = strength_ref[c][:1]
        intensity = image[:, c * tile : (c + 1) * tile] * norm
        resist = jax.nn.sigmoid(STEEP * (strength * intensity - THRESH))
        slope = (resist - goal) * resist * (1.0 - resist)
        slopes.append(slope * (4.0 * STEEP * norm * strength))
    back = dot(gather_rows_ref[...], three_right(jnp.concatenate(slopes, 1)))
    high, low = split(
        jnp.concatenate([back[:, c * tile : (c + 1) * tile] for c in range(conds)], 0), 2
    )
    gh, gl = gather_cols_ref[:tile], gather_cols_ref[tile:]
    slope = dot(jnp.concatenate([high, low, high], 1), jnp.concatenate([gh, gh, gl], 0))

    for pair in range(pairs):
        weight = []
        for k in (2 * pair, 2 * pair + 1):
            weight.append(slope[k // per * count : (k // per + 1) * count])
        at = pair * count
        field_ref[at : at + count, :] = field_ref[at : at + count, :] * jnp.concatenate(weight, 1)
    weights = from_cols_ref[...]
    weights = jnp.concatenate(
        [
            weights,
            jnp.concatenate([weights[:, : 2 * HALF], jnp.zeros((wide, 2 * HALF), BF)], 1),
        ],
        0,
    )
    for at in (0, chunk):
        high, low = split(field_ref[at : at + chunk, :], 2)
        back = dot(jnp.concatenate([high, low], 1), weights)
        rows_ref[at : at + chunk, :] = back[:, : 2 * HALF] + back[:, 2 * HALF :]

    from_rows = from_rows_ref[...]
    sum_one, sum_two = 0.0, 0.0
    for quad in range(pairs // 2):
        at = 2 * quad * count
        value = jnp.concatenate(
            [rows_ref[at : at + count, :], rows_ref[at + count : at + 2 * count, :]], 1
        )
        back = dot(from_rows, three_right(value))
        top, bottom = back[:BAND], back[BAND:]
        one = first_ref[:, quad * wide : (quad + 1) * wide]
        two = second_ref[:, quad * wide : (quad + 1) * wide]
        sum_one = sum_one + (one * top + two * bottom)
        sum_two = sum_two + (two * top - one * bottom)
    sum_one = sum_one[:, : 2 * HALF] + sum_one[:, 2 * HALF :]
    sum_two = sum_two[:, : 2 * HALF] + sum_two[:, 2 * HALF :]
    out_ref[...] = jnp.where(
        lane_ids(sum_one.shape) < HALF,
        sum_one + pltpu.roll(sum_one, HALF, 1),
        sum_two + pltpu.roll(sum_two, HALF, 1),
    )


def adjoint_kernel(mine_ref, theirs_ref, cols_ref, rows_ref, out_hbm, out_ref, sems):
    tile = out_ref.shape[1]
    high, low = split(mine_ref[...] + theirs_ref[...], 2)
    size = cols_ref.shape[0] // 2
    ch, cl = cols_ref[:size], cols_ref[size:]
    halves = dot(jnp.concatenate([high, low, high], 1), jnp.concatenate([ch, ch, cl], 0))
    joined = three_right(jnp.concatenate([halves[:, :tile], halves[:, tile:]], 0))
    count = sems.shape[0]
    step = tile // count
    copies = []
    for at in range(count):
        rows = pl.ds(at * step, step)
        out_ref[rows] = dot(rows_ref[rows], joined)
        copies.append(pltpu.make_async_copy(out_ref.at[rows], out_hbm.at[rows], sems.at[at]))
        copies[-1].start()
    for copy in copies:
        copy.wait()


VMEM = pl.BlockSpec(memory_space=pltpu.VMEM)
SMEM = pl.BlockSpec(memory_space=pltpu.SMEM)
HBM = pl.BlockSpec(memory_space=pltpu.HBM)


def call(body, outs, specs, args, scratch=(), flops=1000000, grant=8, out_spec=None):
    shapes = [
        shape if hasattr(shape, "dtype") else jax.ShapeDtypeStruct(shape, F32) for shape in outs
    ]
    one = len(outs) == 1
    args = [
        pltpu.with_memory_space_constraint(value, pltpu.HBM) if spec is HBM else value
        for spec, value in zip(specs, args)
    ]
    return pl.pallas_call(
        body,
        out_shape=shapes[0] if one else shapes,
        in_specs=specs,
        out_specs=(out_spec or VMEM) if one else [VMEM] * len(outs),
        scratch_shapes=list(scratch),
        compiler_params=pltpu.CompilerParams(vmem_limit_bytes=grant * 2**20),
        cost_estimate=pl.CostEstimate(flops=flops, bytes_accessed=1000000, transcendentals=0),
    )(*args)


def swaps(mesh_shape, along):
    rows, cols, cores = mesh_shape
    out = []
    for r in range(rows):
        for c in range(cols):
            for k in range(cores):
                at, line, size = (r, c, rows) if along == 0 else (c, r, cols)
                other = at + 1 if (k + line) % 2 == 0 else at - 1
                inside = 0 <= other < size
                at, line = (other, line) if inside else (at, line ^ 1)
                to = (at, line) if along == 0 else (line, at)
                if to[0] < rows and to[1] < cols:
                    out.append(((r * cols + c) * cores + k, (to[0] * cols + to[1]) * cores + 1 - k))
    return out


def shards(mesh_shape, mask, target, cond_index, kernels, dose):
    tile = mask.shape[0]
    window = tile + 2 * MARGIN
    swap = [(0, 1), (1, 0)]
    conds = cond_index.shape[0]
    count = kernels.shape[2]
    block = (2 * BAND, 2 * HALF)
    beside = lax.ppermute(mask, AXES, swaps(mesh_shape, 1))
    fetched = local_tables(tile, window) + (target,)
    fetched += field_tables(tile, window) + adjoint_tables(tile, window)
    own, chosen, strength, *fetched = call(
        open_kernel,
        [block, (conds, count, 2, BAND * BAND), (conds, 8, tile)]
        + [jax.ShapeDtypeStruct(value.shape, value.dtype) for value in fetched],
        [HBM] * (4 + len(fetched)),
        (cond_index, dose, mask, jnp.transpose(kernels, (0, 2, 1, 3))) + fetched,
        scratch=[
            pltpu.SMEM(cond_index.shape, jnp.int32),
            pltpu.SMEM(dose.shape, F32),
            pltpu.VMEM(mask.shape, F32),
            pltpu.SemaphoreType.DMA((3 + conds + len(fetched),)),
        ],
    )
    beside, own, chosen, strength, fetched = lax.optimization_barrier(
        (beside, own, chosen, strength, fetched)
    )
    *local, later_target = fetched[:4]
    later = [later_target, *fetched[4:]]
    near = call(
        functools.partial(near_kernel, mesh_shape), [block], [VMEM] * 4, (beside, *local)
    )
    far = lax.ppermute(near, "cond", swap)
    real = chosen[:, :, 0].reshape(conds * count * BAND, BAND)
    imag = chosen[:, :, 1].reshape(conds * count * BAND, BAND)
    far, real, imag = lax.optimization_barrier((far, real, imag))
    message = own[:BAND] + near[:BAND] + far[:BAND]
    side = lax.ppermute(message, AXES, swaps(mesh_shape, 0))
    total = conds * count
    arranged = call(arrange_kernel, [(BAND, total * HALF)] * 2, [VMEM] * 2, (real, imag))
    side, arranged = lax.optimization_barrier((side, arranged))
    other = lax.ppermute(side, "cond", swap)

    cotangent = call(
        functools.partial(field_kernel, mesh_shape),
        [(BAND, 2 * HALF)],
        [VMEM] * 17,
        (strength, own, near, far, side, other, *arranged, *later[:-2]),
        scratch=[
            pltpu.VMEM((total * BAND, 2 * HALF), F32),
            pltpu.VMEM((total * BAND, 4 * HALF), F32),
        ],
    )
    theirs = lax.ppermute(cotangent, "cond", swap)
    return call(
        adjoint_kernel, [(tile, tile)], [VMEM] * 4, (cotangent, theirs, *later[-2:]),
        scratch=[pltpu.VMEM((tile, tile), F32), pltpu.SemaphoreType.DMA((4,))], out_spec=HBM,
    )


def solution(mesh):
    in_specs = (P("row", "col"), P("row", "col"), P("cond"), P(), P())
    out_specs = P("row", "col")
    shape = tuple(mesh.shape[name] for name in AXES)
    body = functools.partial(shards, shape)
    return jax.shard_map(body, mesh=mesh, in_specs=in_specs, out_specs=out_specs, check_vma=False)
```

profile of v0, /device:TPU:0, one launch (start us, length us, event | category | flops | bytes accessed | tf_op | source)
XLA Modules:
  0.0 15.0 jit_solution(7131493119832283230)
XLA Ops:
  0.0 2.5 %collective-permute-start = (f32[128,128]{1,0:T(8,128)}, f32[128,128]{1,0:T(8,128)S(1)}, u32[]{:S(2)}, u32[]{:S(2)}) collective-permute-start(f32[128,128]{1,0:T(8,128)} %refs_2_.1), channel_id=1, source_target_pairs={{0,3},{1,8},{2,5},{3,0},{4,7},{5,2},{6,15},{7,4},{8,1},{9,10},{10,... | collective-permute-start | bytes 196616 | tf_op jit(solution)/shard_map/ppermute | solution.py:444
  2.5 2.1 %shard_map.172 = (f32[48,128]{1,0:T(8,128)S(1)}, f32[2,12,2,576]{3,2,1,0:T(2,128)S(1)}, f32[2,8,128]{2,1,0:T(8,128)S(1)}, bf16[768,128]{1,0:T(8,128)(2,1)S(1)}, ...) custom-call(s32[2]{0:T(128)} %refs_0_.1, ...), custom_call_target="tpu_custom_call" | custom-call | flops 1000000 | bytes 1000000 | tf_op jit(solution)/shard_map/pallas_call | solution.py:410
  4.6 0.1 collective-permute-done.tile_ref
  4.7 0.5 %shard_map.173.near_ref = f32[48,128]{1,0:T(8,128)S(1)} custom-call(f32[128,128]{1,0:T(8,128)S(1)} %collective-permute-done.tile_ref, bf16[768,128]{1,0:T(8,128)(2,1)S(1)} %get-tuple-element.68.col_ref, bf16[48,384]{1,0:T(8,128)(2,1)S(1)} %get-tuple-element.69.row_ref, f32[48,128]{1,0:T(8,128)S(1)} %get-tuple-element.70.turn_ref), custom_call_target="tpu_custom_call" | custom-call | flops 1000000 | bytes 1000000 | tf_op jit(solution)/shard_map/pallas_call | solution.py:410
  5.2 0.6 %collective-permute-start.1 = (f32[48,128]{1,0:T(8,128)S(1)}, f32[48,128]{1,0:T(8,128)S(1)}, u32[]{:S(2)}, u32[]{:S(2)}) collective-permute-start(f32[48,128]{1,0:T(8,128)S(1)} %shard_map.173.near_ref), channel_id=1, source_target_pairs={{0,1},{1,0},{2,3},{3,2},{4,5},{5,4},{6,7},{7,6},{8,9},{9,8},{10,11... | collective-permute-start | bytes 73736 | tf_op jit(solution)/shard_map/ppermute | solution.py:468
  5.8 0.3 %slice_reduce_fusion = (f32[2,12,576]{2,1,0:T(8,128)S(1)}, f32[2,12,576]{2,1,0:T(8,128)S(1)}) fusion(f32[2,12,2,576]{3,2,1,0:T(2,128)S(1)} %get-tuple-element.71), kind=kLoop, calls=%fused_computation | loop fusion | bytes 221184 | tf_op jit(solution)/shard_map/slice | solution.py:470
  6.1 0.1 reshape_squeeze.7.imag_ref
  6.3 0.1 reshape_squeeze.6.real_ref
  6.4 0.2 %collective-permute-done.1.far_ref = f32[48,128]{1,0:T(8,128)S(1)} collective-permute-done((f32[48,128]{1,0:T(8,128)S(1)}, f32[48,128]{1,0:T(8,128)S(1)}, u32[]{:S(2)}, u32[]{:S(2)}) %collective-permute-start.1) | collective-permute-done | bytes 24608 | tf_op jit(solution)/shard_map/ppermute | solution.py:468
  6.6 1.7 %collective-permute-start.2 = (f32[24,128]{1,0:T(8,128)S(1)}, f32[24,128]{1,0:T(8,128)S(1)}, u32[]{:S(2)}, u32[]{:S(2)}) collective-permute-start(f32[24,128]{1,0:T(8,128)S(1)} %fusion), channel_id=1, source_target_pairs={{0,9},{1,2},{2,1},{3,10},{4,13},{5,6},{6,5},{7,14},{8,17},{9,0},{1... | collective-permute-start | bytes 36872 | tf_op jit(solution)/shard_map/ppermute | solution.py:473
  8.4 0.3 %shard_map.174 = (f32[24,1536]{1,0:T(8,128)S(1)}, f32[24,1536]{1,0:T(8,128)S(1)}) custom-call(f32[576,24]{1,0:T(8,128)S(1)} %reshape_squeeze.6.real_ref, f32[576,24]{1,0:T(8,128)S(1)} %reshape_squeeze.7.imag_ref), custom_call_target="tpu_custom_call" | custom-call | flops 1000000 | bytes 1000000 | tf_op jit(solution)/shard_map/pallas_call | solution.py:410
  8.7 1.1 %collective-permute-done.2.side_ref = f32[24,128]{1,0:T(8,128)S(1)} collective-permute-done((f32[24,128]{1,0:T(8,128)S(1)}, f32[24,128]{1,0:T(8,128)S(1)}, u32[]{:S(2)}, u32[]{:S(2)}) %collective-permute-start.2) | collective-permute-done | bytes 12320 | tf_op jit(solution)/shard_map/ppermute | solution.py:473
  9.8 0.4 %collective-permute-start.3 = (f32[24,128]{1,0:T(8,128)S(1)}, f32[24,128]{1,0:T(8,128)S(1)}, u32[]{:S(2)}, u32[]{:S(2)}) collective-permute-start(f32[24,128]{1,0:T(8,128)S(1)} %collective-permute-done.2.side_ref), channel_id=1, source_target_pairs={{0,1},{1,0},{2,3},{3,2},{4,5},{5,4},{6,7},{7,6},{8,9},{9,8},{10,11... | collective-permute-start | bytes 36872 | tf_op jit(solution)/shard_map/ppermute | solution.py:477
  10.2 0.8 %collective-permute-done.3.other_ref = f32[24,128]{1,0:T(8,128)S(1)} collective-permute-done((f32[24,128]{1,0:T(8,128)S(1)}, f32[24,128]{1,0:T(8,128)S(1)}, u32[]{:S(2)}, u32[]{:S(2)}) %collective-permute-start.3) | collective-permute-done | bytes 12320 | tf_op jit(solution)/shard_map/ppermute | solution.py:477
  11.0 1.8 %shard_map.175.mine_ref = f32[24,128]{1,0:T(8,128)S(1)} custom-call(f32[2,8,128]{2,1,0:T(8,128)S(1)} %get-tuple-element.65.strength_ref, f32[48,128]{1,0:T(8,128)S(1)} %get-tuple-element.66.own_ref, f32[48,128]{1,0:T(8,128)S(1)} %shard_map.173.near_ref, f32[48,128]{1,0:T(8,128)S(1)} %collective-permute-done.1.far_ref, ...), custom_call_target="tpu_custom_call" | custom-call | flops 1000000 | bytes 1000000 | tf_op jit(solution)/shard_map/pallas_call | solution.py:410
  12.8 0.4 %collective-permute-start.4 = (f32[24,128]{1,0:T(8,128)S(1)}, f32[24,128]{1,0:T(8,128)S(1)}, u32[]{:S(2)}, u32[]{:S(2)}) collective-permute-start(f32[24,128]{1,0:T(8,128)S(1)} %shard_map.175.mine_ref), channel_id=1, source_target_pairs={{0,1},{1,0},{2,3},{3,2},{4,5},{5,4},{6,7},{7,6},{8,9},{9,8},{10,11... | collective-permute-start | bytes 36872 | tf_op jit(solution)/shard_map/ppermute | solution.py:489
  13.2 0.8 %collective-permute-done.4.theirs_ref = f32[24,128]{1,0:T(8,128)S(1)} collective-permute-done((f32[24,128]{1,0:T(8,128)S(1)}, f32[24,128]{1,0:T(8,128)S(1)}, u32[]{:S(2)}, u32[]{:S(2)}) %collective-permute-start.4) | collective-permute-done | bytes 12320 | tf_op jit(solution)/shard_map/ppermute | solution.py:489
  14.0 1.0 %shard_map.176 = f32[128,128]{1,0:T(8,128)} custom-call(f32[24,128]{1,0:T(8,128)S(1)} %shard_map.175.mine_ref, f32[24,128]{1,0:T(8,128)S(1)} %collective-permute-done.4.theirs_ref, bf16[256,256]{1,0:T(8,128)(2,1)S(1)} %get-tuple-element.89.cols_ref, bf16[128,144]{1,0:T(8,128)(2,1)S(1)} %get-tuple-element.90.rows_ref), custom_call_target="tpu_custom_call" | custom-call | flops 1000000 | bytes 1000000 | tf_op jit(solution)/shard_map/pallas_call | solution.py:410
  (1 shorter events, 0.0 us)
Async XLA Ops:
  0.0 4.7 %collective-permute-start = (f32[128,128]{1,0:T(8,128)}, f32[128,128]{1,0:T(8,128)S(1)}, u32[]{:S(2)}, u32[]{:S(2)}) collective-permute-start(f32[128,128]{1,0:T(8,128)} %refs_2_.1), channel_id=1, source_target_pairs={{0,3},{1,8},{2,5},{3,0},{4,7},{5,2},{6,15},{7,4},{8,1},{9,10},{10,... | collective-permute-start | bytes 196616 | tf_op jit(solution)/shard_map/ppermute | solution.py:444
  5.2 1.4 %collective-permute-start.1 = (f32[48,128]{1,0:T(8,128)S(1)}, f32[48,128]{1,0:T(8,128)S(1)}, u32[]{:S(2)}, u32[]{:S(2)}) collective-permute-start(f32[48,128]{1,0:T(8,128)S(1)} %shard_map.173.near_ref), channel_id=1, source_target_pairs={{0,1},{1,0},{2,3},{3,2},{4,5},{5,4},{6,7},{7,6},{8,9},{9,8},{10,11... | collective-permute-start | bytes 73736 | tf_op jit(solution)/shard_map/ppermute | solution.py:468
  6.6 3.2 %collective-permute-start.2 = (f32[24,128]{1,0:T(8,128)S(1)}, f32[24,128]{1,0:T(8,128)S(1)}, u32[]{:S(2)}, u32[]{:S(2)}) collective-permute-start(f32[24,128]{1,0:T(8,128)S(1)} %fusion), channel_id=1, source_target_pairs={{0,9},{1,2},{2,1},{3,10},{4,13},{5,6},{6,5},{7,14},{8,17},{9,0},{1... | collective-permute-start | bytes 36872 | tf_op jit(solution)/shard_map/ppermute | solution.py:473
  9.8 1.2 %collective-permute-start.3 = (f32[24,128]{1,0:T(8,128)S(1)}, f32[24,128]{1,0:T(8,128)S(1)}, u32[]{:S(2)}, u32[]{:S(2)}) collective-permute-start(f32[24,128]{1,0:T(8,128)S(1)} %collective-permute-done.2.side_ref), channel_id=1, source_target_pairs={{0,1},{1,0},{2,3},{3,2},{4,5},{5,4},{6,7},{7,6},{8,9},{9,8},{10,11... | collective-permute-start | bytes 36872 | tf_op jit(solution)/shard_map/ppermute | solution.py:477
  12.8 1.2 %collective-permute-start.4 = (f32[24,128]{1,0:T(8,128)S(1)}, f32[24,128]{1,0:T(8,128)S(1)}, u32[]{:S(2)}, u32[]{:S(2)}) collective-permute-start(f32[24,128]{1,0:T(8,128)S(1)} %shard_map.175.mine_ref), channel_id=1, source_target_pairs={{0,1},{1,0},{2,3},{3,2},{4,5},{5,4},{6,7},{7,6},{8,9},{9,8},{10,11... | collective-permute-start | bytes 36872 | tf_op jit(solution)/shard_map/ppermute | solution.py:489
where the time goes:
time: 15.3 us; the launch traced here: 15 us
  Pallas kernels  5.65 us (37%)
  starting transfers between devices  5.59 us (37%)
  waiting for transfers between devices  3.13 us (20%)
  local copies, waits for them, and re-layouts  0.62 us (4%)
    pallas_call x5, Pallas kernels, call(): pl.pallas_call(body, out_shape=shapes[0] if one else shapes, in_specs=spe...  5.65 us
    ppermute x1, starting transfers between devices, shards(): beside = lax.ppermute(mask, AXES, swaps(mesh_shape, 1))  2.49 us
    ppermute x1, starting transfers between devices, shards(): side = lax.ppermute(message, AXES, swaps(mesh_shape, 0))  1.74 us
    ppermute x1, waiting for transfers between devices, shards(): side = lax.ppermute(message, AXES, swaps(mesh_shape, 0))  1.11 us
    ppermute x1, waiting for transfers between devices, shards(): other = lax.ppermute(side, 'cond', swap)  0.83 us
    ppermute x1, waiting for transfers between devices, shards(): theirs = lax.ppermute(cotangent, 'cond', swap)  0.83 us
    ppermute x1, starting transfers between devices, shards(): far = lax.ppermute(near, 'cond', swap)  0.59 us
    ppermute x1, starting transfers between devices, shards(): other = lax.ppermute(side, 'cond', swap)  0.4 us
  transfers between devices with their start and end apart: 5, of which 5 were waited for; matrix products, arithmetic and copies ran while one was open for 4% of the time, Pallas kernels for 16%

commit v1 on v0

--- a/solution.py
+++ b/solution.py
@@ -1,5 +1,6 @@
 import functools
 import math
+from itertools import zip_longest
 
 import jax
 import jax.numpy as jnp
@@ -179,7 +180,7 @@
     size = col_table.shape[0] // 2
     high, low = split(tile_value, 2)
     ch, cl = col_table[:size], col_table[size:]
-    partial = dot(jnp.concatenate([high, low, high], 1), jnp.concatenate([ch, ch, cl], 0))
+    partial = dot(jnp.concatenate([high, low], 1), jnp.concatenate([ch, ch], 0)) + dot(high, cl)
     both = dot(row_table, three_right(partial))
     lane = lane_ids((BAND, both.shape[1])) % HALF
 
@@ -264,8 +265,7 @@
 ):
     conds = strength_ref.shape[0]
     count = 2 * BAND
-    pairs = first_ref.shape[1] // (2 * HALF)
-    per = 2 * pairs // conds
+    per = first_ref.shape[1] // HALF // conds
     tile = target_ref.shape[0]
     wide = 4 * HALF
     row, col, core = (lax.axis_index(name) for name in AXES)
@@ -286,87 +286,88 @@
     imag = imag + pltpu.roll(imag, 2 * HALF - BAND, 1)
 
     to_rows = to_rows_ref[...]
-    for quad in range(pairs // 2):
-        blocks = []
-        for pair in (2 * quad, 2 * quad + 1):
-            one = first_ref[:, pair * 2 * HALF : (pair + 1) * 2 * HALF]
-            two = second_ref[:, pair * 2 * HALF : (pair + 1) * 2 * HALF]
-            blocks.append(jnp.concatenate([one * real + two * imag, one * imag - two * real], 0))
-        both = dot(to_rows, three_right(jnp.concatenate(blocks, 1)))
-        for part in range(2):
-            at = (2 * quad + part) * count
-            rows_ref[at : at + count, :] = both[:, part * 2 * HALF : (part + 1) * 2 * HALF]
-
-    weights = four_weights(to_cols_ref)
-    chunk = rows_ref.shape[0] // 2
-    for at in (0, chunk):
-        high, low = split(rows_ref[at : at + chunk, :], 2)
-        field_ref[at : at + chunk, :] = dot(jnp.concatenate([high, low, high, low], 1), weights)
-    sums = [jnp.zeros((count, 2 * HALF), F32) for _ in range(conds)]
-    for pair in range(pairs):
-        both = field_ref[pair * count : (pair + 1) * count, :]
-        squares = both * both
-        for part in range(2):
-            c = (2 * pair + part) // per
-            sums[c] = sums[c] + squares[:, part * 2 * HALF : (part + 1) * 2 * HALF]
-
-    coarse = jnp.concatenate([value + pltpu.roll(value, HALF, 1) for value in sums], 0)
-    lines = dot(doubled(coarse), four_weights(spread_cols_ref))
-    right = jnp.concatenate(
-        [three_right(lines[c * count : (c + 1) * count]) for c in range(conds)], 1
-    )
-    image = dot(spread_ref[...], right)
-
+    to_cols = four_weights(to_cols_ref)
+    spread_cols = four_weights(spread_cols_ref)
+    gather_cols = gather_cols_ref[...]
+    gather_cols = jnp.concatenate([gather_cols[:tile], gather_cols], 0)
+    from_cols = from_cols_ref[...]
+    from_cols = jnp.concatenate(
+        [
+            from_cols,
+            jnp.concatenate([from_cols[:, : 2 * HALF], jnp.zeros((wide, 2 * HALF), BF)], 1),
+        ],
+        0,
+    )
+    from_rows = from_rows_ref[...]
     goal = target_ref[...].astype(F32)
     norm = 1.0 / (per * BAND * BAND)
-    slopes = []
-    for c in range(conds):
+    pairs = per // 2
+
+    def pair_lanes(ref, pair, width=1):
+        return ref[:, pair * 2 * HALF : (pair + width) * 2 * HALF]
+
+    def condition(c, sums):
+        first, last = c * pairs, (c + 1) * pairs
+        for quad in range(first, last, 2):
+            blocks = []
+            for pair in (quad, quad + 1):
+                one, two = pair_lanes(first_ref, pair), pair_lanes(second_ref, pair)
+                blocks.append(
+                    jnp.concatenate([one * real + two * imag, one * imag - two * real], 0)
+                )
+            both = dot(to_rows, three_right(jnp.concatenate(blocks, 1)))
+            rows_ref[quad * count : (quad + 1) * count, :] = both[:, : 2 * HALF]
+            rows_ref[(quad + 1) * count : (quad + 2) * count, :] = both[:, 2 * HALF :]
+            yield
+        total = 0.0
+        rows = slice(first * count, last * count)
+        high, low = split(rows_ref[rows, :], 2)
+        field_ref[rows, :] = dot(jnp.concatenate([high, low, high, low], 1), to_cols)
+        for pair in range(first, last):
+            both = field_ref[pair * count : (pair + 1) * count, :]
+            squares = both * both
+            total = total + (squares[:, : 2 * HALF] + squares[:, 2 * HALF :])
+        yield
+        coarse = total + pltpu.roll(total, HALF, 1)
+        lines = dot(doubled(coarse), spread_cols)
+        yield
+        intensity = dot(spread_ref[...], three_right(lines)) * norm
         strength = strength_ref[c][:1]
-        intensity = image[:, c * tile : (c + 1) * tile] * norm
         resist = jax.nn.sigmoid(STEEP * (strength * intensity - THRESH))
         slope = (resist - goal) * resist * (1.0 - resist)
-        slopes.append(slope * (4.0 * STEEP * norm * strength))
-    back = dot(gather_rows_ref[...], three_right(jnp.concatenate(slopes, 1)))
-    high, low = split(
-        jnp.concatenate([back[:, c * tile : (c + 1) * tile] for c in range(conds)], 0), 2
-    )
-    gh, gl = gather_cols_ref[:tile], gather_cols_ref[tile:]
-    slope = dot(jnp.concatenate([high, low, high], 1), jnp.concatenate([gh, gh, gl], 0))
-
-    for pair in range(pairs):
-        weight = []
-        for k in (2 * pair, 2 * pair + 1):
-            weight.append(slope[k // per * count : (k // per + 1) * count])
-        at = pair * count
-        field_ref[at : at + count, :] = field_ref[at : at + count, :] * jnp.concatenate(weight, 1)
-    weights = from_cols_ref[...]
-    weights = jnp.concatenate(
-        [
-            weights,
-            jnp.concatenate([weights[:, : 2 * HALF], jnp.zeros((wide, 2 * HALF), BF)], 1),
-        ],
-        0,
-    )
-    for at in (0, chunk):
-        high, low = split(field_ref[at : at + chunk, :], 2)
-        back = dot(jnp.concatenate([high, low], 1), weights)
-        rows_ref[at : at + chunk, :] = back[:, : 2 * HALF] + back[:, 2 * HALF :]
-
-    from_rows = from_rows_ref[...]
-    sum_one, sum_two = 0.0, 0.0
-    for quad in range(pairs // 2):
-        at = 2 * quad * count
-        value = jnp.concatenate(
-            [rows_ref[at : at + count, :], rows_ref[at + count : at + 2 * count, :]], 1
-        )
-        back = dot(from_rows, three_right(value))
-        top, bottom = back[:BAND], back[BAND:]
-        one = first_ref[:, quad * wide : (quad + 1) * wide]
-        two = second_ref[:, quad * wide : (quad + 1) * wide]
-        sum_one = sum_one + (one * top + two * bottom)
-        sum_two = sum_two + (two * top - one * bottom)
-    sum_one = sum_one[:, : 2 * HALF] + sum_one[:, 2 * HALF :]
-    sum_two = sum_two[:, : 2 * HALF] + sum_two[:, 2 * HALF :]
+        slope = slope * (4.0 * STEEP * norm * strength)
+        yield
+        back = dot(gather_rows_ref[...], three_right(slope))
+        yield
+        high, low = split(back, 2)
+        slope = dot(jnp.concatenate([high, low, high], 1), gather_cols)
+        slope = jnp.concatenate([slope, slope], 1)
+        yield
+        for pair in range(first, last):
+            part = slice(pair * count, (pair + 1) * count)
+            field_ref[part, :] = field_ref[part, :] * slope
+        back = dot(jnp.concatenate(split(field_ref[rows, :], 2), 1), from_cols)
+        rows_ref[rows, :] = back[:, : 2 * HALF] + back[:, 2 * HALF :]
+        yield
+        for quad in range(first, last, 2):
+            value = jnp.concatenate(
+                [
+                    rows_ref[quad * count : (quad + 1) * count, :],
+                    rows_ref[(quad + 1) * count : (quad + 2) * count, :],
+                ],
+                1,
+            )
+            back = dot(from_rows, three_right(value))
+            top, bottom = back[:BAND], back[BAND:]
+            one, two = pair_lanes(first_ref, quad, 2), pair_lanes(second_ref, quad, 2)
+            sums[0] = sums[0] + (one * top + two * bottom)
+            sums[1] = sums[1] + (two * top - one * bottom)
+            yield
+
+    sums = [0.0, 0.0]
+    for _ in zip_longest(*(condition(c, sums) for c in range(conds))):
+        pass
+    sum_one, sum_two = (value[:, : 2 * HALF] + value[:, 2 * HALF :] for value in sums)
     out_ref[...] = jnp.where(
         lane_ids(sum_one.shape) < HALF,
         sum_one + pltpu.roll(sum_one, HALF, 1),
@@ -374,23 +375,14 @@
     )
 
 
-def adjoint_kernel(mine_ref, theirs_ref, cols_ref, rows_ref, out_hbm, out_ref, sems):
+def adjoint_kernel(mine_ref, theirs_ref, cols_ref, rows_ref, out_ref):
     tile = out_ref.shape[1]
     high, low = split(mine_ref[...] + theirs_ref[...], 2)
     size = cols_ref.shape[0] // 2
     ch, cl = cols_ref[:size], cols_ref[size:]
     halves = dot(jnp.concatenate([high, low, high], 1), jnp.concatenate([ch, ch, cl], 0))
-    joined = three_right(jnp.concatenate([halves[:, :tile], halves[:, tile:]], 0))
-    count = sems.shape[0]
-    step = tile // count
-    copies = []
-    for at in range(count):
-        rows = pl.ds(at * step, step)
-        out_ref[rows] = dot(rows_ref[rows], joined)
-        copies.append(pltpu.make_async_copy(out_ref.at[rows], out_hbm.at[rows], sems.at[at]))
-        copies[-1].start()
-    for copy in copies:
-        copy.wait()
+    joined = jnp.concatenate([halves[:, :tile], halves[:, tile:]], 0)
+    out_ref[...] = dot(rows_ref[...], three_right(joined))
 
 
 VMEM = pl.BlockSpec(memory_space=pltpu.VMEM)
@@ -398,7 +390,7 @@
 HBM = pl.BlockSpec(memory_space=pltpu.HBM)
 
 
-def call(body, outs, specs, args, scratch=(), flops=1000000, grant=8, out_spec=None):
+def call(body, outs, specs, args, scratch=(), flops=1000000, grant=8):
     shapes = [
         shape if hasattr(shape, "dtype") else jax.ShapeDtypeStruct(shape, F32) for shape in outs
     ]
@@ -411,7 +403,7 @@
         body,
         out_shape=shapes[0] if one else shapes,
         in_specs=specs,
-        out_specs=(out_spec or VMEM) if one else [VMEM] * len(outs),
+        out_specs=VMEM if one else [VMEM] * len(outs),
         scratch_shapes=list(scratch),
         compiler_params=pltpu.CompilerParams(vmem_limit_bytes=grant * 2**20),
         cost_estimate=pl.CostEstimate(flops=flops, bytes_accessed=1000000, transcendentals=0),
@@ -488,8 +480,7 @@
     )
     theirs = lax.ppermute(cotangent, "cond", swap)
     return call(
-        adjoint_kernel, [(tile, tile)], [VMEM] * 4, (cotangent, theirs, *later[-2:]),
-        scratch=[pltpu.VMEM((tile, tile), F32), pltpu.SemaphoreType.DMA((4,))], out_spec=HBM,
+        adjoint_kernel, [(tile, tile)], [VMEM] * 4, (cotangent, theirs, *later[-2:])
     )
 
 

time: 15.3 us -> 15.2 us (level)
  no operation moved by 1% of the time
where the time goes in v1:
time: 15.2 us; the launch traced here: 14.9 us
  starting transfers between devices  5.62 us (37%)
  Pallas kernels  5.53 us (36%)
  waiting for transfers between devices  3.13 us (21%)
  local copies, waits for them, and re-layouts  0.62 us (4%)
    pallas_call x5, Pallas kernels, call(): pl.pallas_call(body, out_shape=shapes[0] if one else shapes, in_specs=spe...  5.53 us
    ppermute x1, starting transfers between devices, shards(): beside = lax.ppermute(mask, AXES, swaps(mesh_shape, 1))  2.49 us
    ppermute x1, starting transfers between devices, shards(): side = lax.ppermute(message, AXES, swaps(mesh_shape, 0))  1.75 us
    ppermute x1, waiting for transfers between devices, shards(): side = lax.ppermute(message, AXES, swaps(mesh_shape, 0))  1.11 us
    ppermute x1, waiting for transfers between devices, shards(): other = lax.ppermute(side, 'cond', swap)  0.83 us
    ppermute x1, waiting for transfers between devices, shards(): theirs = lax.ppermute(cotangent, 'cond', swap)  0.83 us
    ppermute x1, starting transfers between devices, shards(): far = lax.ppermute(near, 'cond', swap)  0.59 us
    ppermute x1, starting transfers between devices, shards(): other = lax.ppermute(side, 'cond', swap)  0.4 us
  transfers between devices with their start and end apart: 5, of which 5 were waited for; matrix products, arithmetic and copies ran while one was open for 4% of the time, Pallas kernels for 16%

profile of v1, /device:TPU:0, one launch (start us, length us, event | category | flops | bytes accessed | tf_op | source)
XLA Modules:
  0.0 14.9 jit_solution(17967349747140115389)
XLA Ops:
  0.0 2.5 %collective-permute-start = (f32[128,128]{1,0:T(8,128)}, f32[128,128]{1,0:T(8,128)S(1)}, u32[]{:S(2)}, u32[]{:S(2)}) collective-permute-start(f32[128,128]{1,0:T(8,128)} %refs_2_.1), channel_id=1, source_target_pairs={{0,3},{1,8},{2,5},{3,0},{4,7},{5,2},{6,15},{7,4},{8,1},{9,10},{10,... | collective-permute-start | bytes 196616 | tf_op jit(solution)/shard_map/ppermute | solution.py:436
  2.5 2.1 %shard_map.172 = (f32[48,128]{1,0:T(8,128)S(1)}, f32[2,12,2,576]{3,2,1,0:T(2,128)S(1)}, f32[2,8,128]{2,1,0:T(8,128)S(1)}, bf16[768,128]{1,0:T(8,128)(2,1)S(1)}, ...) custom-call(s32[2]{0:T(128)} %refs_0_.1, ...), custom_call_target="tpu_custom_call" | custom-call | flops 1000000 | bytes 1000000 | tf_op jit(solution)/shard_map/pallas_call | solution.py:402
  4.6 0.1 collective-permute-done.tile_ref
  4.7 0.5 %shard_map.173.near_ref = f32[48,128]{1,0:T(8,128)S(1)} custom-call(f32[128,128]{1,0:T(8,128)S(1)} %collective-permute-done.tile_ref, bf16[768,128]{1,0:T(8,128)(2,1)S(1)} %get-tuple-element.68.col_ref, bf16[48,384]{1,0:T(8,128)(2,1)S(1)} %get-tuple-element.69.row_ref, f32[48,128]{1,0:T(8,128)S(1)} %get-tuple-element.70.turn_ref), custom_call_target="tpu_custom_call" | custom-call | flops 1000000 | bytes 1000000 | tf_op jit(solution)/shard_map/pallas_call | solution.py:402
  5.2 0.6 %collective-permute-start.1 = (f32[48,128]{1,0:T(8,128)S(1)}, f32[48,128]{1,0:T(8,128)S(1)}, u32[]{:S(2)}, u32[]{:S(2)}) collective-permute-start(f32[48,128]{1,0:T(8,128)S(1)} %shard_map.173.near_ref), channel_id=1, source_target_pairs={{0,1},{1,0},{2,3},{3,2},{4,5},{5,4},{6,7},{7,6},{8,9},{9,8},{10,11... | collective-permute-start | bytes 73736 | tf_op jit(solution)/shard_map/ppermute | solution.py:460
  5.8 0.3 %slice_reduce_fusion = (f32[2,12,576]{2,1,0:T(8,128)S(1)}, f32[2,12,576]{2,1,0:T(8,128)S(1)}) fusion(f32[2,12,2,576]{3,2,1,0:T(2,128)S(1)} %get-tuple-element.71), kind=kLoop, calls=%fused_computation | loop fusion | bytes 221184 | tf_op jit(solution)/shard_map/slice | solution.py:462
  6.1 0.1 reshape_squeeze.7.imag_ref
  6.2 0.1 reshape_squeeze.6.real_ref
  6.4 0.2 %collective-permute-done.1.far_ref = f32[48,128]{1,0:T(8,128)S(1)} collective-permute-done((f32[48,128]{1,0:T(8,128)S(1)}, f32[48,128]{1,0:T(8,128)S(1)}, u32[]{:S(2)}, u32[]{:S(2)}) %collective-permute-start.1) | collective-permute-done | bytes 24608 | tf_op jit(solution)/shard_map/ppermute | solution.py:460
  6.6 1.7 %collective-permute-start.2 = (f32[24,128]{1,0:T(8,128)S(1)}, f32[24,128]{1,0:T(8,128)S(1)}, u32[]{:S(2)}, u32[]{:S(2)}) collective-permute-start(f32[24,128]{1,0:T(8,128)S(1)} %fusion), channel_id=1, source_target_pairs={{0,9},{1,2},{2,1},{3,10},{4,13},{5,6},{6,5},{7,14},{8,17},{9,0},{1... | collective-permute-start | bytes 36872 | tf_op jit(solution)/shard_map/ppermute | solution.py:465
  8.4 0.3 %shard_map.174 = (f32[24,1536]{1,0:T(8,128)S(1)}, f32[24,1536]{1,0:T(8,128)S(1)}) custom-call(f32[576,24]{1,0:T(8,128)S(1)} %reshape_squeeze.6.real_ref, f32[576,24]{1,0:T(8,128)S(1)} %reshape_squeeze.7.imag_ref), custom_call_target="tpu_custom_call" | custom-call | flops 1000000 | bytes 1000000 | tf_op jit(solution)/shard_map/pallas_call | solution.py:402
  8.7 1.1 %collective-permute-done.2.side_ref = f32[24,128]{1,0:T(8,128)S(1)} collective-permute-done((f32[24,128]{1,0:T(8,128)S(1)}, f32[24,128]{1,0:T(8,128)S(1)}, u32[]{:S(2)}, u32[]{:S(2)}) %collective-permute-start.2) | collective-permute-done | bytes 12320 | tf_op jit(solution)/shard_map/ppermute | solution.py:465
  9.8 0.4 %collective-permute-start.3 = (f32[24,128]{1,0:T(8,128)S(1)}, f32[24,128]{1,0:T(8,128)S(1)}, u32[]{:S(2)}, u32[]{:S(2)}) collective-permute-start(f32[24,128]{1,0:T(8,128)S(1)} %collective-permute-done.2.side_ref), channel_id=1, source_target_pairs={{0,1},{1,0},{2,3},{3,2},{4,5},{5,4},{6,7},{7,6},{8,9},{9,8},{10,11... | collective-permute-start | bytes 36872 | tf_op jit(solution)/shard_map/ppermute | solution.py:469
  10.2 0.8 %collective-permute-done.3.other_ref = f32[24,128]{1,0:T(8,128)S(1)} collective-permute-done((f32[24,128]{1,0:T(8,128)S(1)}, f32[24,128]{1,0:T(8,128)S(1)}, u32[]{:S(2)}, u32[]{:S(2)}) %collective-permute-start.3) | collective-permute-done | bytes 12320 | tf_op jit(solution)/shard_map/ppermute | solution.py:469
  11.0 1.7 %shard_map.175.mine_ref = f32[24,128]{1,0:T(8,128)S(1)} custom-call(f32[2,8,128]{2,1,0:T(8,128)S(1)} %get-tuple-element.65.strength_ref, f32[48,128]{1,0:T(8,128)S(1)} %get-tuple-element.66.own_ref, f32[48,128]{1,0:T(8,128)S(1)} %shard_map.173.near_ref, f32[48,128]{1,0:T(8,128)S(1)} %collective-permute-done.1.far_ref, ...), custom_call_target="tpu_custom_call" | custom-call | flops 1000000 | bytes 1000000 | tf_op jit(solution)/shard_map/pallas_call | solution.py:402
  12.8 0.4 %collective-permute-start.4 = (f32[24,128]{1,0:T(8,128)S(1)}, f32[24,128]{1,0:T(8,128)S(1)}, u32[]{:S(2)}, u32[]{:S(2)}) collective-permute-start(f32[24,128]{1,0:T(8,128)S(1)} %shard_map.175.mine_ref), channel_id=1, source_target_pairs={{0,1},{1,0},{2,3},{3,2},{4,5},{5,4},{6,7},{7,6},{8,9},{9,8},{10,11... | collective-permute-start | bytes 36872 | tf_op jit(solution)/shard_map/ppermute | solution.py:481
  13.2 0.8 %collective-permute-done.4.theirs_ref = f32[24,128]{1,0:T(8,128)S(1)} collective-permute-done((f32[24,128]{1,0:T(8,128)S(1)}, f32[24,128]{1,0:T(8,128)S(1)}, u32[]{:S(2)}, u32[]{:S(2)}) %collective-permute-start.4) | collective-permute-done | bytes 12320 | tf_op jit(solution)/shard_map/ppermute | solution.py:481
  14.0 1.0 %shard_map.176 = f32[128,128]{1,0:T(8,128)} custom-call(f32[24,128]{1,0:T(8,128)S(1)} %shard_map.175.mine_ref, f32[24,128]{1,0:T(8,128)S(1)} %collective-permute-done.4.theirs_ref, bf16[256,256]{1,0:T(8,128)(2,1)S(1)} %get-tuple-element.89.cols_ref, bf16[128,144]{1,0:T(8,128)(2,1)S(1)} %get-tuple-element.90.rows_ref), custom_call_target="tpu_custom_call" | custom-call | flops 1000000 | bytes 1000000 | tf_op jit(solution)/shard_map/pallas_call | solution.py:402
  (1 shorter events, 0.0 us)
Async XLA Ops:
  0.0 4.7 %collective-permute-start = (f32[128,128]{1,0:T(8,128)}, f32[128,128]{1,0:T(8,128)S(1)}, u32[]{:S(2)}, u32[]{:S(2)}) collective-permute-start(f32[128,128]{1,0:T(8,128)} %refs_2_.1), channel_id=1, source_target_pairs={{0,3},{1,8},{2,5},{3,0},{4,7},{5,2},{6,15},{7,4},{8,1},{9,10},{10,... | collective-permute-start | bytes 196616 | tf_op jit(solution)/shard_map/ppermute | solution.py:436
  5.2 1.4 %collective-permute-start.1 = (f32[48,128]{1,0:T(8,128)S(1)}, f32[48,128]{1,0:T(8,128)S(1)}, u32[]{:S(2)}, u32[]{:S(2)}) collective-permute-start(f32[48,128]{1,0:T(8,128)S(1)} %shard_map.173.near_ref), channel_id=1, source_target_pairs={{0,1},{1,0},{2,3},{3,2},{4,5},{5,4},{6,7},{7,6},{8,9},{9,8},{10,11... | collective-permute-start | bytes 73736 | tf_op jit(solution)/shard_map/ppermute | solution.py:460
  6.6 3.2 %collective-permute-start.2 = (f32[24,128]{1,0:T(8,128)S(1)}, f32[24,128]{1,0:T(8,128)S(1)}, u32[]{:S(2)}, u32[]{:S(2)}) collective-permute-start(f32[24,128]{1,0:T(8,128)S(1)} %fusion), channel_id=1, source_target_pairs={{0,9},{1,2},{2,1},{3,10},{4,13},{5,6},{6,5},{7,14},{8,17},{9,0},{1... | collective-permute-start | bytes 36872 | tf_op jit(solution)/shard_map/ppermute | solution.py:465
  9.8 1.2 %collective-permute-start.3 = (f32[24,128]{1,0:T(8,128)S(1)}, f32[24,128]{1,0:T(8,128)S(1)}, u32[]{:S(2)}, u32[]{:S(2)}) collective-permute-start(f32[24,128]{1,0:T(8,128)S(1)} %collective-permute-done.2.side_ref), channel_id=1, source_target_pairs={{0,1},{1,0},{2,3},{3,2},{4,5},{5,4},{6,7},{7,6},{8,9},{9,8},{10,11... | collective-permute-start | bytes 36872 | tf_op jit(solution)/shard_map/ppermute | solution.py:469
  12.8 1.2 %collective-permute-start.4 = (f32[24,128]{1,0:T(8,128)S(1)}, f32[24,128]{1,0:T(8,128)S(1)}, u32[]{:S(2)}, u32[]{:S(2)}) collective-permute-start(f32[24,128]{1,0:T(8,128)S(1)} %shard_map.175.mine_ref), channel_id=1, source_target_pairs={{0,1},{1,0},{2,3},{3,2},{4,5},{5,4},{6,7},{7,6},{8,9},{9,8},{10,11... | collective-permute-start | bytes 36872 | tf_op jit(solution)/shard_map/ppermute | solution.py:481

commit v2 on v1

--- a/solution.py
+++ b/solution.py
@@ -258,8 +258,30 @@
         second_ref[:, pair * 2 * HALF : (pair + 1) * 2 * HALF] = second
 
 
+def row_block(mesh_shape, value, core):
+    row, col, _ = (lax.axis_index(name) for name in AXES)
+    onward, valid = toward(row, core, col, mesh_shape[0])
+    low_half = lane_ids(value.shape) < HALF
+    kept = jnp.where(onward, jnp.where(low_half, 0.0, value), jnp.where(low_half, value, 0.0))
+    kept = jnp.where(valid, kept, 0.0)
+    return kept + pltpu.roll(kept, HALF, 1)
+
+
+def spread_lanes(value):
+    lane = lane_ids(value.shape) % HALF
+    real = jnp.where(lane < BAND, value, 0.0)
+    imag = jnp.where(lane >= BAND, value, 0.0)
+    return real + pltpu.roll(real, BAND, 1), imag + pltpu.roll(imag, 2 * HALF - BAND, 1)
+
+
+def base_kernel(mesh_shape, own_ref, near_ref, far_ref, side_ref, out_ref):
+    value = own_ref[BAND:] + near_ref[BAND:] + far_ref[BAND:]
+    value += row_block(mesh_shape, side_ref[...], lax.axis_index("cond"))
+    out_ref[:BAND], out_ref[BAND:] = spread_lanes(value)
+
+
 def field_kernel(
-    mesh_shape, strength_ref, own_ref, near_ref, far_ref, side_ref, other_ref,
+    mesh_shape, strength_ref, base_ref, other_ref,
     first_ref, second_ref, target_ref, to_cols_ref, to_rows_ref, spread_cols_ref, spread_ref,
     gather_rows_ref, gather_cols_ref, from_rows_ref, from_cols_ref, out_ref, rows_ref, field_ref,
 ):
@@ -268,25 +290,13 @@
     per = first_ref.shape[1] // HALF // conds
     tile = target_ref.shape[0]
     wide = 4 * HALF
-    row, col, core = (lax.axis_index(name) for name in AXES)
-
-    def half(value, core):
-        onward, valid = toward(row, core, col, mesh_shape[0])
-        low_half = lane_ids(value.shape) < HALF
-        kept = jnp.where(onward, jnp.where(low_half, 0.0, value), jnp.where(low_half, value, 0.0))
-        kept = jnp.where(valid, kept, 0.0)
-        return kept + pltpu.roll(kept, HALF, 1)
-
-    spectrum = own_ref[BAND:] + near_ref[BAND:] + far_ref[BAND:]
-    spectrum += half(side_ref[...], core) + half(other_ref[...], 1 - core)
-    lane = lane_ids(spectrum.shape) % HALF
-    real = jnp.where(lane < BAND, spectrum, 0.0)
-    imag = jnp.where(lane >= BAND, spectrum, 0.0)
-    real = real + pltpu.roll(real, BAND, 1)
-    imag = imag + pltpu.roll(imag, 2 * HALF - BAND, 1)
+    core = lax.axis_index("cond")
+    real, imag = spread_lanes(row_block(mesh_shape, other_ref[...], 1 - core))
+    real, imag = base_ref[:BAND] + real, base_ref[BAND:] + imag
 
     to_rows = to_rows_ref[...]
-    to_cols = four_weights(to_cols_ref)
+    th, tl = to_cols_ref[: 2 * HALF], to_cols_ref[2 * HALF :]
+    to_cols = jnp.concatenate([th, th, tl], 0)
     spread_cols = four_weights(spread_cols_ref)
     gather_cols = gather_cols_ref[...]
     gather_cols = jnp.concatenate([gather_cols[:tile], gather_cols], 0)
@@ -322,7 +332,7 @@
         total = 0.0
         rows = slice(first * count, last * count)
         high, low = split(rows_ref[rows, :], 2)
-        field_ref[rows, :] = dot(jnp.concatenate([high, low, high, low], 1), to_cols)
+        field_ref[rows, :] = dot(jnp.concatenate([high, low, high], 1), to_cols)
         for pair in range(first, last):
             both = field_ref[pair * count : (pair + 1) * count, :]
             squares = both * both
@@ -467,12 +477,16 @@
     arranged = call(arrange_kernel, [(BAND, total * HALF)] * 2, [VMEM] * 2, (real, imag))
     side, arranged = lax.optimization_barrier((side, arranged))
     other = lax.ppermute(side, "cond", swap)
+    base = call(
+        functools.partial(base_kernel, mesh_shape), [block], [VMEM] * 4, (own, near, far, side)
+    )
+    other, base = lax.optimization_barrier((other, base))
 
     cotangent = call(
         functools.partial(field_kernel, mesh_shape),
         [(BAND, 2 * HALF)],
-        [VMEM] * 17,
-        (strength, own, near, far, side, other, *arranged, *later[:-2]),
+        [VMEM] * 14,
+        (strength, base, other, *arranged, *later[:-2]),
         scratch=[
             pltpu.VMEM((total * BAND, 2 * HALF), F32),
             pltpu.VMEM((total * BAND, 4 * HALF), F32),

time: 15.2 us -> 15.2 us (level)
    pallas_call x5 -> x6, Pallas kernels: 5.53 us -> 5.68 us  [call(): pl.pallas_call(body, out_shape=shapes[0] if one else shapes, in_specs=spe...]
  transfers between devices with their start and end apart: 5 -> 5, of which waited for: 5 -> 5; matrix products, arithmetic and copies ran while one was open for 4% -> 4% of each run, Pallas kernels for 16% -> 17%
where the time goes in v2:
time: 15.2 us; the launch traced here: 14.9 us
  Pallas kernels  5.68 us (37%)
  starting transfers between devices  5.61 us (37%)
  waiting for transfers between devices  2.98 us (20%)
  local copies, waits for them, and re-layouts  0.62 us (4%)
    pallas_call x6, Pallas kernels, call(): pl.pallas_call(body, out_shape=shapes[0] if one else shapes, in_specs=spe...  5.68 us
    ppermute x1, starting transfers between devices, shards(): beside = lax.ppermute(mask, AXES, swaps(mesh_shape, 1))  2.49 us
    ppermute x1, starting transfers between devices, shards(): side = lax.ppermute(message, AXES, swaps(mesh_shape, 0))  1.75 us
    ppermute x1, waiting for transfers between devices, shards(): side = lax.ppermute(message, AXES, swaps(mesh_shape, 0))  1.11 us
    ppermute x1, waiting for transfers between devices, shards(): theirs = lax.ppermute(cotangent, 'cond', swap)  0.84 us
    ppermute x1, waiting for transfers between devices, shards(): other = lax.ppermute(side, 'cond', swap)  0.68 us
    ppermute x1, starting transfers between devices, shards(): far = lax.ppermute(near, 'cond', swap)  0.59 us
    ppermute x1, starting transfers between devices, shards(): other = lax.ppermute(side, 'cond', swap)  0.4 us
  transfers between devices with their start and end apart: 5, of which 5 were waited for; matrix products, arithmetic and copies ran while one was open for 4% of the time, Pallas kernels for 17%

profile of v2, /device:TPU:0, one launch (start us, length us, event | category | flops | bytes accessed | tf_op | source)
XLA Modules:
  0.0 14.9 jit_solution(15056090689444445950)
XLA Ops:
  0.0 2.5 %collective-permute-start = (f32[128,128]{1,0:T(8,128)}, f32[128,128]{1,0:T(8,128)S(1)}, u32[]{:S(2)}, u32[]{:S(2)}) collective-permute-start(f32[128,128]{1,0:T(8,128)} %refs_2_.1), channel_id=1, source_target_pairs={{0,3},{1,8},{2,5},{3,0},{4,7},{5,2},{6,15},{7,4},{8,1},{9,10},{10,... | collective-permute-start | bytes 196616 | tf_op jit(solution)/shard_map/ppermute | solution.py:446
  2.5 2.1 %shard_map.172 = (f32[48,128]{1,0:T(8,128)S(1)}, f32[2,12,2,576]{3,2,1,0:T(2,128)S(1)}, f32[2,8,128]{2,1,0:T(8,128)S(1)}, bf16[768,128]{1,0:T(8,128)(2,1)S(1)}, ...) custom-call(s32[2]{0:T(128)} %refs_0_.1, ...), custom_call_target="tpu_custom_call" | custom-call | flops 1000000 | bytes 1000000 | tf_op jit(solution)/shard_map/pallas_call | solution.py:412
  4.6 0.1 collective-permute-done.tile_ref
  4.7 0.5 %shard_map.173.near_ref = f32[48,128]{1,0:T(8,128)S(1)} custom-call(f32[128,128]{1,0:T(8,128)S(1)} %collective-permute-done.tile_ref, bf16[768,128]{1,0:T(8,128)(2,1)S(1)} %get-tuple-element.70.col_ref, bf16[48,384]{1,0:T(8,128)(2,1)S(1)} %get-tuple-element.71.row_ref, f32[48,128]{1,0:T(8,128)S(1)} %get-tuple-element.72.turn_ref), custom_call_target="tpu_custom_call" | custom-call | flops 1000000 | bytes 1000000 | tf_op jit(solution)/shard_map/pallas_call | solution.py:412
  5.2 0.6 %collective-permute-start.1 = (f32[48,128]{1,0:T(8,128)S(1)}, f32[48,128]{1,0:T(8,128)S(1)}, u32[]{:S(2)}, u32[]{:S(2)}) collective-permute-start(f32[48,128]{1,0:T(8,128)S(1)} %shard_map.173.near_ref), channel_id=1, source_target_pairs={{0,1},{1,0},{2,3},{3,2},{4,5},{5,4},{6,7},{7,6},{8,9},{9,8},{10,11... | collective-permute-start | bytes 73736 | tf_op jit(solution)/shard_map/ppermute | solution.py:470
  5.8 0.3 %slice_reduce_fusion = (f32[2,12,576]{2,1,0:T(8,128)S(1)}, f32[2,12,576]{2,1,0:T(8,128)S(1)}) fusion(f32[2,12,2,576]{3,2,1,0:T(2,128)S(1)} %get-tuple-element.73), kind=kLoop, calls=%fused_computation | loop fusion | bytes 221184 | tf_op jit(solution)/shard_map/slice | solution.py:472
  6.1 0.1 reshape_squeeze.7.imag_ref
  6.2 0.1 reshape_squeeze.6.real_ref
  6.4 0.2 %collective-permute-done.1.far_ref = f32[48,128]{1,0:T(8,128)S(1)} collective-permute-done((f32[48,128]{1,0:T(8,128)S(1)}, f32[48,128]{1,0:T(8,128)S(1)}, u32[]{:S(2)}, u32[]{:S(2)}) %collective-permute-start.1) | collective-permute-done | bytes 24608 | tf_op jit(solution)/shard_map/ppermute | solution.py:470
  6.6 1.7 %collective-permute-start.2 = (f32[24,128]{1,0:T(8,128)S(1)}, f32[24,128]{1,0:T(8,128)S(1)}, u32[]{:S(2)}, u32[]{:S(2)}) collective-permute-start(f32[24,128]{1,0:T(8,128)S(1)} %fusion), channel_id=1, source_target_pairs={{0,9},{1,2},{2,1},{3,10},{4,13},{5,6},{6,5},{7,14},{8,17},{9,0},{1... | collective-permute-start | bytes 36872 | tf_op jit(solution)/shard_map/ppermute | solution.py:475
  8.4 0.3 %shard_map.174 = (f32[24,1536]{1,0:T(8,128)S(1)}, f32[24,1536]{1,0:T(8,128)S(1)}) custom-call(f32[576,24]{1,0:T(8,128)S(1)} %reshape_squeeze.6.real_ref, f32[576,24]{1,0:T(8,128)S(1)} %reshape_squeeze.7.imag_ref), custom_call_target="tpu_custom_call" | custom-call | flops 1000000 | bytes 1000000 | tf_op jit(solution)/shard_map/pallas_call | solution.py:412
  8.7 1.1 %collective-permute-done.2.side_ref = f32[24,128]{1,0:T(8,128)S(1)} collective-permute-done((f32[24,128]{1,0:T(8,128)S(1)}, f32[24,128]{1,0:T(8,128)S(1)}, u32[]{:S(2)}, u32[]{:S(2)}) %collective-permute-start.2) | collective-permute-done | bytes 12320 | tf_op jit(solution)/shard_map/ppermute | solution.py:475
  9.8 0.4 %collective-permute-start.3 = (f32[24,128]{1,0:T(8,128)S(1)}, f32[24,128]{1,0:T(8,128)S(1)}, u32[]{:S(2)}, u32[]{:S(2)}) collective-permute-start(f32[24,128]{1,0:T(8,128)S(1)} %collective-permute-done.2.side_ref), channel_id=1, source_target_pairs={{0,1},{1,0},{2,3},{3,2},{4,5},{5,4},{6,7},{7,6},{8,9},{9,8},{10,11... | collective-permute-start | bytes 36872 | tf_op jit(solution)/shard_map/ppermute | solution.py:479
  10.2 0.1 %shard_map.175.base_ref = f32[48,128]{1,0:T(8,128)S(1)} custom-call(f32[48,128]{1,0:T(8,128)S(1)} %get-tuple-element.68.own_ref, f32[48,128]{1,0:T(8,128)S(1)} %shard_map.173.near_ref, f32[48,128]{1,0:T(8,128)S(1)} %collective-permute-done.1.far_ref, f32[24,128]{1,0:T(8,128)S(1)} %collective-permute-done.2.side_ref), custom_call_target="tpu_custom_call" | custom-call | flops 1000000 | bytes 1000000 | tf_op jit(solution)/shard_map/pallas_call | solution.py:412
  10.3 0.7 %collective-permute-done.3.other_ref = f32[24,128]{1,0:T(8,128)S(1)} collective-permute-done((f32[24,128]{1,0:T(8,128)S(1)}, f32[24,128]{1,0:T(8,128)S(1)}, u32[]{:S(2)}, u32[]{:S(2)}) %collective-permute-start.3) | collective-permute-done | bytes 12320 | tf_op jit(solution)/shard_map/ppermute | solution.py:479
  11.0 1.7 %shard_map.176.mine_ref = f32[24,128]{1,0:T(8,128)S(1)} custom-call(f32[2,8,128]{2,1,0:T(8,128)S(1)} %get-tuple-element.67.strength_ref, f32[48,128]{1,0:T(8,128)S(1)} %shard_map.175.base_ref, f32[24,128]{1,0:T(8,128)S(1)} %collective-permute-done.3.other_ref, f32[24,1536]{1,0:T(8,128)S(1)} %get-tuple-element.82.first_ref, ...), custom_call_target="tpu_custom_call" | custom-call | flops 1000000 | bytes 1000000 | tf_op jit(solution)/shard_map/pallas_call | solution.py:412
  12.8 0.4 %collective-permute-start.4 = (f32[24,128]{1,0:T(8,128)S(1)}, f32[24,128]{1,0:T(8,128)S(1)}, u32[]{:S(2)}, u32[]{:S(2)}) collective-permute-start(f32[24,128]{1,0:T(8,128)S(1)} %shard_map.176.mine_ref), channel_id=1, source_target_pairs={{0,1},{1,0},{2,3},{3,2},{4,5},{5,4},{6,7},{7,6},{8,9},{9,8},{10,11... | collective-permute-start | bytes 36872 | tf_op jit(solution)/shard_map/ppermute | solution.py:495
  13.1 0.8 %collective-permute-done.4.theirs_ref = f32[24,128]{1,0:T(8,128)S(1)} collective-permute-done((f32[24,128]{1,0:T(8,128)S(1)}, f32[24,128]{1,0:T(8,128)S(1)}, u32[]{:S(2)}, u32[]{:S(2)}) %collective-permute-start.4) | collective-permute-done | bytes 12320 | tf_op jit(solution)/shard_map/ppermute | solution.py:495
  14.0 1.0 %shard_map.177 = f32[128,128]{1,0:T(8,128)} custom-call(f32[24,128]{1,0:T(8,128)S(1)} %shard_map.176.mine_ref, f32[24,128]{1,0:T(8,128)S(1)} %collective-permute-done.4.theirs_ref, bf16[256,256]{1,0:T(8,128)(2,1)S(1)} %get-tuple-element.93.cols_ref, bf16[128,144]{1,0:T(8,128)(2,1)S(1)} %get-tuple-element.94.rows_ref), custom_call_target="tpu_custom_call" | custom-call | flops 1000000 | bytes 1000000 | tf_op jit(solution)/shard_map/pallas_call | solution.py:412
  (1 shorter events, 0.0 us)
Async XLA Ops:
  0.0 4.7 %collective-permute-start = (f32[128,128]{1,0:T(8,128)}, f32[128,128]{1,0:T(8,128)S(1)}, u32[]{:S(2)}, u32[]{:S(2)}) collective-permute-start(f32[128,128]{1,0:T(8,128)} %refs_2_.1), channel_id=1, source_target_pairs={{0,3},{1,8},{2,5},{3,0},{4,7},{5,2},{6,15},{7,4},{8,1},{9,10},{10,... | collective-permute-start | bytes 196616 | tf_op jit(solution)/shard_map/ppermute | solution.py:446
  5.2 1.4 %collective-permute-start.1 = (f32[48,128]{1,0:T(8,128)S(1)}, f32[48,128]{1,0:T(8,128)S(1)}, u32[]{:S(2)}, u32[]{:S(2)}) collective-permute-start(f32[48,128]{1,0:T(8,128)S(1)} %shard_map.173.near_ref), channel_id=1, source_target_pairs={{0,1},{1,0},{2,3},{3,2},{4,5},{5,4},{6,7},{7,6},{8,9},{9,8},{10,11... | collective-permute-start | bytes 73736 | tf_op jit(solution)/shard_map/ppermute | solution.py:470
  6.6 3.2 %collective-permute-start.2 = (f32[24,128]{1,0:T(8,128)S(1)}, f32[24,128]{1,0:T(8,128)S(1)}, u32[]{:S(2)}, u32[]{:S(2)}) collective-permute-start(f32[24,128]{1,0:T(8,128)S(1)} %fusion), channel_id=1, source_target_pairs={{0,9},{1,2},{2,1},{3,10},{4,13},{5,6},{6,5},{7,14},{8,17},{9,0},{1... | collective-permute-start | bytes 36872 | tf_op jit(solution)/shard_map/ppermute | solution.py:475
  9.8 1.2 %collective-permute-start.3 = (f32[24,128]{1,0:T(8,128)S(1)}, f32[24,128]{1,0:T(8,128)S(1)}, u32[]{:S(2)}, u32[]{:S(2)}) collective-permute-start(f32[24,128]{1,0:T(8,128)S(1)} %collective-permute-done.2.side_ref), channel_id=1, source_target_pairs={{0,1},{1,0},{2,3},{3,2},{4,5},{5,4},{6,7},{7,6},{8,9},{9,8},{10,11... | collective-permute-start | bytes 36872 | tf_op jit(solution)/shard_map/ppermute | solution.py:479
  12.8 1.2 %collective-permute-start.4 = (f32[24,128]{1,0:T(8,128)S(1)}, f32[24,128]{1,0:T(8,128)S(1)}, u32[]{:S(2)}, u32[]{:S(2)}) collective-permute-start(f32[24,128]{1,0:T(8,128)S(1)} %shard_map.176.mine_ref), channel_id=1, source_target_pairs={{0,1},{1,0},{2,3},{3,2},{4,5},{5,4},{6,7},{7,6},{8,9},{9,8},{10,11... | collective-permute-start | bytes 36872 | tf_op jit(solution)/shard_map/ppermute | solution.py:495

commit v3 on v2

--- a/solution.py
+++ b/solution.py
@@ -375,7 +375,11 @@
             yield
 
     sums = [0.0, 0.0]
-    for _ in zip_longest(*(condition(c, sums) for c in range(conds))):
+    steps = [condition(c, sums) for c in range(conds)]
+    for step in steps:
+        for _ in range(pairs // 2):
+            next(step)
+    for _ in zip_longest(*steps):
         pass
     sum_one, sum_two = (value[:, : 2 * HALF] + value[:, 2 * HALF :] for value in sums)
     out_ref[...] = jnp.where(

time: 15.2 us -> 15.2 us (level)
  no operation moved by 1% of the time
where the time goes in v3:
time: 15.2 us; the launch traced here: 14.9 us
  Pallas kernels  5.67 us (37%)
  starting transfers between devices  5.61 us (37%)
  waiting for transfers between devices  2.98 us (20%)
  local copies, waits for them, and re-layouts  0.62 us (4%)
    pallas_call x6, Pallas kernels, call(): pl.pallas_call(body, out_shape=shapes[0] if one else shapes, in_specs=spe...  5.67 us
    ppermute x1, starting transfers between devices, shards(): beside = lax.ppermute(mask, AXES, swaps(mesh_shape, 1))  2.49 us
    ppermute x1, starting transfers between devices, shards(): side = lax.ppermute(message, AXES, swaps(mesh_shape, 0))  1.75 us
    ppermute x1, waiting for transfers between devices, shards(): side = lax.ppermute(message, AXES, swaps(mesh_shape, 0))  1.11 us
    ppermute x1, waiting for transfers between devices, shards(): theirs = lax.ppermute(cotangent, 'cond', swap)  0.83 us
    ppermute x1, waiting for transfers between devices, shards(): other = lax.ppermute(side, 'cond', swap)  0.68 us
    ppermute x1, starting transfers between devices, shards(): far = lax.ppermute(near, 'cond', swap)  0.59 us
    ppermute x1, starting transfers between devices, shards(): other = lax.ppermute(side, 'cond', swap)  0.4 us
  transfers between devices with their start and end apart: 5, of which 5 were waited for; matrix products, arithmetic and copies ran while one was open for 4% of the time, Pallas kernels for 17%

profile of v3, /device:TPU:0, one launch (start us, length us, event | category | flops | bytes accessed | tf_op | source)
XLA Modules:
  0.0 14.9 jit_solution(6364424508436443638)
XLA Ops:
  0.0 2.5 %collective-permute-start = (f32[128,128]{1,0:T(8,128)}, f32[128,128]{1,0:T(8,128)S(1)}, u32[]{:S(2)}, u32[]{:S(2)}) collective-permute-start(f32[128,128]{1,0:T(8,128)} %refs_2_.1), channel_id=1, source_target_pairs={{0,3},{1,8},{2,5},{3,0},{4,7},{5,2},{6,15},{7,4},{8,1},{9,10},{10,... | collective-permute-start | bytes 196616 | tf_op jit(solution)/shard_map/ppermute | solution.py:450
  2.5 2.1 %shard_map.172 = (f32[48,128]{1,0:T(8,128)S(1)}, f32[2,12,2,576]{3,2,1,0:T(2,128)S(1)}, f32[2,8,128]{2,1,0:T(8,128)S(1)}, bf16[768,128]{1,0:T(8,128)(2,1)S(1)}, ...) custom-call(s32[2]{0:T(128)} %refs_0_.1, ...), custom_call_target="tpu_custom_call" | custom-call | flops 1000000 | bytes 1000000 | tf_op jit(solution)/shard_map/pallas_call | solution.py:416
  4.6 0.1 collective-permute-done.tile_ref
  4.7 0.5 %shard_map.173.near_ref = f32[48,128]{1,0:T(8,128)S(1)} custom-call(f32[128,128]{1,0:T(8,128)S(1)} %collective-permute-done.tile_ref, bf16[768,128]{1,0:T(8,128)(2,1)S(1)} %get-tuple-element.70.col_ref, bf16[48,384]{1,0:T(8,128)(2,1)S(1)} %get-tuple-element.71.row_ref, f32[48,128]{1,0:T(8,128)S(1)} %get-tuple-element.72.turn_ref), custom_call_target="tpu_custom_call" | custom-call | flops 1000000 | bytes 1000000 | tf_op jit(solution)/shard_map/pallas_call | solution.py:416
  5.2 0.6 %collective-permute-start.1 = (f32[48,128]{1,0:T(8,128)S(1)}, f32[48,128]{1,0:T(8,128)S(1)}, u32[]{:S(2)}, u32[]{:S(2)}) collective-permute-start(f32[48,128]{1,0:T(8,128)S(1)} %shard_map.173.near_ref), channel_id=1, source_target_pairs={{0,1},{1,0},{2,3},{3,2},{4,5},{5,4},{6,7},{7,6},{8,9},{9,8},{10,11... | collective-permute-start | bytes 73736 | tf_op jit(solution)/shard_map/ppermute | solution.py:474
  5.8 0.3 %slice_reduce_fusion = (f32[2,12,576]{2,1,0:T(8,128)S(1)}, f32[2,12,576]{2,1,0:T(8,128)S(1)}) fusion(f32[2,12,2,576]{3,2,1,0:T(2,128)S(1)} %get-tuple-element.73), kind=kLoop, calls=%fused_computation | loop fusion | bytes 221184 | tf_op jit(solution)/shard_map/slice | solution.py:476
  6.1 0.1 reshape_squeeze.7.imag_ref
  6.2 0.1 reshape_squeeze.6.real_ref
  6.4 0.2 %collective-permute-done.1.far_ref = f32[48,128]{1,0:T(8,128)S(1)} collective-permute-done((f32[48,128]{1,0:T(8,128)S(1)}, f32[48,128]{1,0:T(8,128)S(1)}, u32[]{:S(2)}, u32[]{:S(2)}) %collective-permute-start.1) | collective-permute-done | bytes 24608 | tf_op jit(solution)/shard_map/ppermute | solution.py:474
  6.6 1.7 %collective-permute-start.2 = (f32[24,128]{1,0:T(8,128)S(1)}, f32[24,128]{1,0:T(8,128)S(1)}, u32[]{:S(2)}, u32[]{:S(2)}) collective-permute-start(f32[24,128]{1,0:T(8,128)S(1)} %fusion), channel_id=1, source_target_pairs={{0,9},{1,2},{2,1},{3,10},{4,13},{5,6},{6,5},{7,14},{8,17},{9,0},{1... | collective-permute-start | bytes 36872 | tf_op jit(solution)/shard_map/ppermute | solution.py:479
  8.4 0.3 %shard_map.174 = (f32[24,1536]{1,0:T(8,128)S(1)}, f32[24,1536]{1,0:T(8,128)S(1)}) custom-call(f32[576,24]{1,0:T(8,128)S(1)} %reshape_squeeze.6.real_ref, f32[576,24]{1,0:T(8,128)S(1)} %reshape_squeeze.7.imag_ref), custom_call_target="tpu_custom_call" | custom-call | flops 1000000 | bytes 1000000 | tf_op jit(solution)/shard_map/pallas_call | solution.py:416
  8.7 1.1 %collective-permute-done.2.side_ref = f32[24,128]{1,0:T(8,128)S(1)} collective-permute-done((f32[24,128]{1,0:T(8,128)S(1)}, f32[24,128]{1,0:T(8,128)S(1)}, u32[]{:S(2)}, u32[]{:S(2)}) %collective-permute-start.2) | collective-permute-done | bytes 12320 | tf_op jit(solution)/shard_map/ppermute | solution.py:479
  9.8 0.4 %collective-permute-start.3 = (f32[24,128]{1,0:T(8,128)S(1)}, f32[24,128]{1,0:T(8,128)S(1)}, u32[]{:S(2)}, u32[]{:S(2)}) collective-permute-start(f32[24,128]{1,0:T(8,128)S(1)} %collective-permute-done.2.side_ref), channel_id=1, source_target_pairs={{0,1},{1,0},{2,3},{3,2},{4,5},{5,4},{6,7},{7,6},{8,9},{9,8},{10,11... | collective-permute-start | bytes 36872 | tf_op jit(solution)/shard_map/ppermute | solution.py:483
  10.2 0.1 %shard_map.175.base_ref = f32[48,128]{1,0:T(8,128)S(1)} custom-call(f32[48,128]{1,0:T(8,128)S(1)} %get-tuple-element.68.own_ref, f32[48,128]{1,0:T(8,128)S(1)} %shard_map.173.near_ref, f32[48,128]{1,0:T(8,128)S(1)} %collective-permute-done.1.far_ref, f32[24,128]{1,0:T(8,128)S(1)} %collective-permute-done.2.side_ref), custom_call_target="tpu_custom_call" | custom-call | flops 1000000 | bytes 1000000 | tf_op jit(solution)/shard_map/pallas_call | solution.py:416
  10.3 0.7 %collective-permute-done.3.other_ref = f32[24,128]{1,0:T(8,128)S(1)} collective-permute-done((f32[24,128]{1,0:T(8,128)S(1)}, f32[24,128]{1,0:T(8,128)S(1)}, u32[]{:S(2)}, u32[]{:S(2)}) %collective-permute-start.3) | collective-permute-done | bytes 12320 | tf_op jit(solution)/shard_map/ppermute | solution.py:483
  11.0 1.7 %shard_map.176.mine_ref = f32[24,128]{1,0:T(8,128)S(1)} custom-call(f32[2,8,128]{2,1,0:T(8,128)S(1)} %get-tuple-element.67.strength_ref, f32[48,128]{1,0:T(8,128)S(1)} %shard_map.175.base_ref, f32[24,128]{1,0:T(8,128)S(1)} %collective-permute-done.3.other_ref, f32[24,1536]{1,0:T(8,128)S(1)} %get-tuple-element.82.first_ref, ...), custom_call_target="tpu_custom_call" | custom-call | flops 1000000 | bytes 1000000 | tf_op jit(solution)/shard_map/pallas_call | solution.py:416
  12.8 0.4 %collective-permute-start.4 = (f32[24,128]{1,0:T(8,128)S(1)}, f32[24,128]{1,0:T(8,128)S(1)}, u32[]{:S(2)}, u32[]{:S(2)}) collective-permute-start(f32[24,128]{1,0:T(8,128)S(1)} %shard_map.176.mine_ref), channel_id=1, source_target_pairs={{0,1},{1,0},{2,3},{3,2},{4,5},{5,4},{6,7},{7,6},{8,9},{9,8},{10,11... | collective-permute-start | bytes 36872 | tf_op jit(solution)/shard_map/ppermute | solution.py:499
  13.1 0.8 %collective-permute-done.4.theirs_ref = f32[24,128]{1,0:T(8,128)S(1)} collective-permute-done((f32[24,128]{1,0:T(8,128)S(1)}, f32[24,128]{1,0:T(8,128)S(1)}, u32[]{:S(2)}, u32[]{:S(2)}) %collective-permute-start.4) | collective-permute-done | bytes 12320 | tf_op jit(solution)/shard_map/ppermute | solution.py:499
  14.0 1.0 %shard_map.177 = f32[128,128]{1,0:T(8,128)} custom-call(f32[24,128]{1,0:T(8,128)S(1)} %shard_map.176.mine_ref, f32[24,128]{1,0:T(8,128)S(1)} %collective-permute-done.4.theirs_ref, bf16[256,256]{1,0:T(8,128)(2,1)S(1)} %get-tuple-element.93.cols_ref, bf16[128,144]{1,0:T(8,128)(2,1)S(1)} %get-tuple-element.94.rows_ref), custom_call_target="tpu_custom_call" | custom-call | flops 1000000 | bytes 1000000 | tf_op jit(solution)/shard_map/pallas_call | solution.py:416
  (1 shorter events, 0.0 us)
Async XLA Ops:
  0.0 4.7 %collective-permute-start = (f32[128,128]{1,0:T(8,128)}, f32[128,128]{1,0:T(8,128)S(1)}, u32[]{:S(2)}, u32[]{:S(2)}) collective-permute-start(f32[128,128]{1,0:T(8,128)} %refs_2_.1), channel_id=1, source_target_pairs={{0,3},{1,8},{2,5},{3,0},{4,7},{5,2},{6,15},{7,4},{8,1},{9,10},{10,... | collective-permute-start | bytes 196616 | tf_op jit(solution)/shard_map/ppermute | solution.py:450
  5.2 1.4 %collective-permute-start.1 = (f32[48,128]{1,0:T(8,128)S(1)}, f32[48,128]{1,0:T(8,128)S(1)}, u32[]{:S(2)}, u32[]{:S(2)}) collective-permute-start(f32[48,128]{1,0:T(8,128)S(1)} %shard_map.173.near_ref), channel_id=1, source_target_pairs={{0,1},{1,0},{2,3},{3,2},{4,5},{5,4},{6,7},{7,6},{8,9},{9,8},{10,11... | collective-permute-start | bytes 73736 | tf_op jit(solution)/shard_map/ppermute | solution.py:474
  6.6 3.2 %collective-permute-start.2 = (f32[24,128]{1,0:T(8,128)S(1)}, f32[24,128]{1,0:T(8,128)S(1)}, u32[]{:S(2)}, u32[]{:S(2)}) collective-permute-start(f32[24,128]{1,0:T(8,128)S(1)} %fusion), channel_id=1, source_target_pairs={{0,9},{1,2},{2,1},{3,10},{4,13},{5,6},{6,5},{7,14},{8,17},{9,0},{1... | collective-permute-start | bytes 36872 | tf_op jit(solution)/shard_map/ppermute | solution.py:479
  9.8 1.2 %collective-permute-start.3 = (f32[24,128]{1,0:T(8,128)S(1)}, f32[24,128]{1,0:T(8,128)S(1)}, u32[]{:S(2)}, u32[]{:S(2)}) collective-permute-start(f32[24,128]{1,0:T(8,128)S(1)} %collective-permute-done.2.side_ref), channel_id=1, source_target_pairs={{0,1},{1,0},{2,3},{3,2},{4,5},{5,4},{6,7},{7,6},{8,9},{9,8},{10,11... | collective-permute-start | bytes 36872 | tf_op jit(solution)/shard_map/ppermute | solution.py:483
  12.8 1.2 %collective-permute-start.4 = (f32[24,128]{1,0:T(8,128)S(1)}, f32[24,128]{1,0:T(8,128)S(1)}, u32[]{:S(2)}, u32[]{:S(2)}) collective-permute-start(f32[24,128]{1,0:T(8,128)S(1)} %shard_map.176.mine_ref), channel_id=1, source_target_pairs={{0,1},{1,0},{2,3},{3,2},{4,5},{5,4},{6,7},{7,6},{8,9},{9,8},{10,11... | collective-permute-start | bytes 36872 | tf_op jit(solution)/shard_map/ppermute | solution.py:499
